TPU v7x, 32 devices: a whole 2x2x4 slice. The times are simulated.
32 devices in a mesh: dp: 4 (over z), vocab: 8 (over y, x, core).
Axes of the slice: x: 2, y: 2, z: 4, core: 2. Of those that a mesh axis runs over, the one named last changes fastest.
Arguments:
- hidden: bfloat16 [4096, 4096], P(('dp', 'vocab')), may hold values from -4 to 4
- output_weight: bfloat16 [4096, 8192], P(None, 'vocab'), may hold values from -0.09375 to 0.09375
- owners: int32 [4096, 3], P(('dp', 'vocab')), may hold values from 0 to 7, all different within a row; in each aligned block of 128 rows (0 to 127, 128 to 255, ...) at most 64 rows name the same one
- negatives: int32 [4096, 3, 2], P(('dp', 'vocab')), may hold values from 0 to 7
- negative_mask: int32 [4096, 3, 2], P(('dp', 'vocab')), may hold values 0 or 1
- target_block: int32 [4096], P(('dp', 'vocab')), may hold values from 0 to 7
- target_word: int32 [4096], P(('dp', 'vocab')), may hold values from 0 to 127
- log_norm: bfloat16 [4096], P(('dp', 'vocab')), may hold values from 1 to 2
- cotangent: bfloat16 [4096], P(('dp', 'vocab')), may hold values from 4 to 8
Outputs:
- hidden_grad: bfloat16 [4096, 4096], P(('dp', 'vocab'))
- weight_grad: bfloat16 [4096, 8192], P('dp', 'vocab')
Inputs may be any that keep to these rules, and one draw needn't show every extreme that they name: Each row names 3 different owners; among the 128 rows of one device no owner is named by more than 64 rows, and in some device's rows an owner is named by exactly 64.
All inputs are finite; a program needn't handle non-finite values. No bound on the sum of `negative_mask` on one device may be relied on, other than what follows from the above.
Results may differ from a plain program's by a relative error of at most 0.015.
Values may be sent and summed in bfloat16 or wider, within the bound.
A program may use at most 128 MiB of HBM per device.

v0:
```python
import jax
import jax.numpy as jnp
from jax import lax
from jax.sharding import PartitionSpec as P

BLOCK = 128
BLK_DEV = 8
F32 = jnp.float32
BF16 = jnp.bfloat16


def body(
    hidden,
    output_weight,
    owners,
    negatives,
    negative_mask,
    target_block,
    target_word,
    log_norm,
    cotangent,
):
    tokens, width = hidden.shape
    visits = owners.shape[1]
    per_own = negatives.shape[2]
    n_vocab = lax.axis_size("vocab")
    n_dp = lax.axis_size("dp")
    me = lax.axis_index("vocab")
    my_dp = lax.axis_index("dp")
    words = output_weight.shape[1]
    capacity = max(2, tokens * visits * 4 // (3 * n_vocab))
    slots = n_vocab * capacity
    part = width // n_dp
    facts = jnp.concatenate(
        [
            owners.T,
            negatives.reshape(tokens, -1).T,
            negative_mask.reshape(tokens, -1).T,
            target_block[None, :],
            target_word[None, :],
        ],
        axis=0,
    ).astype(BF16)
    facts = jnp.concatenate([facts, log_norm[None, :], cotangent[None, :]], axis=0)
    facts = lax.all_gather(facts, ("dp", "vocab"), axis=0, tiled=False)
    blocks = n_dp * n_vocab
    group_rows = lax.all_gather(hidden, "vocab", axis=0, tiled=False)
    part_rows = lax.all_to_all(hidden, "dp", split_axis=1, concat_axis=0, tiled=True)
    part_rows = lax.all_gather(part_rows.reshape(n_dp, tokens, part), "vocab", axis=1)
    f = facts.astype(F32)
    pairs = visits * per_own
    hit = f[:, :visits, :] == me.astype(F32)
    neg = f[:, visits : visits + pairs, :]
    mask = f[:, visits + pairs : visits + 2 * pairs, :]
    base = visits + 2 * pairs
    t_block, t_word, norm, cot = (f[:, base + i, :] for i in range(4))
    named = jnp.any(hit, axis=1)
    cand = [jnp.where(hit[:, 0], t_block + 1.0, 0.0)]
    for n in range(per_own):
        value = jnp.zeros_like(t_block)
        for v in range(visits):
            i = v * per_own + n
            value = jnp.where(hit[:, v] & (mask[:, i] == 1.0), neg[:, i] + 1.0, value)
        cand.append(value)
    only = []
    for k, value in enumerate(cand):
        for earlier in cand[:k]:
            value = jnp.where(value == earlier, 0.0, value)
        only.append(value)
    upper = jnp.triu(jnp.ones((tokens, tokens), BF16), 1)
    rank = jnp.dot(named.astype(BF16), upper, preferred_element_type=F32)
    place = jnp.where(named, rank, -1.0)
    pick = (
        place[:, None, :] == jnp.arange(capacity, dtype=jnp.int32).astype(F32)[None, :, None]
    ).astype(BF16)
    attrs = jnp.stack(cand + only + [t_word, norm, cot], axis=1).astype(BF16)
    slot_facts = jnp.einsum("sct,sat->sca", pick, attrs, preferred_element_type=F32)
    kinds = per_own + 1
    all_only = slot_facts[:, :, kinds : 2 * kinds].reshape(n_dp * slots, kinds)
    mine = lax.dynamic_slice_in_dim(slot_facts, my_dp * n_vocab, n_vocab, 0).reshape(slots, -1)
    my_pick = lax.dynamic_slice_in_dim(pick, my_dp * n_vocab, n_vocab, 0)
    rows = jnp.einsum("sct,sth->sch", my_pick, group_rows, preferred_element_type=F32)
    rows = rows.astype(BF16).reshape(slots, width)
    scores = jnp.dot(rows, output_weight, preferred_element_type=F32)
    word_ids = jnp.arange(words, dtype=jnp.int32)[None, :]
    word_block = (word_ids // BLOCK + 1).astype(F32)
    word_in = (word_ids % BLOCK).astype(F32)
    counts = jnp.zeros((slots, words), F32)
    for k in range(kinds):
        counts = counts + jnp.where(mine[:, k : k + 1] == word_block, 1.0, 0.0)
    hot = jnp.where(
        (mine[:, 0:1] == word_block) & (mine[:, 2 * kinds : 2 * kinds + 1] == word_in), 1.0, 0.0
    )
    norm_col = mine[:, 2 * kinds + 1 : 2 * kinds + 2]
    cot_col = mine[:, 2 * kinds + 2 : 2 * kinds + 3]
    grown = jnp.where(counts > 0.0, counts * jnp.exp(scores - norm_col), 0.0)
    grad = (cot_col * (grown - hot)).astype(BF16)
    packed = []
    for k in range(kinds):
        which = mine[:, kinds + k : kinds + k + 1]
        value = jnp.zeros((slots, BLOCK), BF16)
        for b in range(BLK_DEV):
            value = jnp.where(which == b + 1.0, grad[:, b * BLOCK : (b + 1) * BLOCK], value)
        packed.append(value)
    packed = jnp.concatenate(packed, axis=1)
    packed = lax.all_gather(packed, "dp", axis=0, tiled=True)
    back = lax.dot_general(
        grad, output_weight, (((1,), (1,)), ((), ())), preferred_element_type=F32
    ).astype(BF16)
    back = jnp.einsum(
        "sct,sch->sth", my_pick, back.reshape(n_vocab, capacity, width), preferred_element_type=F32
    ).astype(BF16)
    hidden_grad = lax.psum_scatter(
        back.reshape(n_vocab * tokens, width), "vocab", scatter_dimension=0, tiled=True
    )
    part_slots = (
        jnp.einsum(
            "sct,sth->sch",
            pick,
            part_rows.reshape(blocks, tokens, part),
            preferred_element_type=F32,
        )
        .astype(BF16)
        .reshape(n_dp * slots, part)
    )
    spread = []
    for b in range(BLK_DEV):
        value = jnp.zeros((n_dp * slots, BLOCK), BF16)
        for k in range(kinds):
            value = jnp.where(
                all_only[:, k : k + 1] == b + 1.0, packed[:, k * BLOCK : (k + 1) * BLOCK], value
            )
        spread.append(value)
    spread = jnp.concatenate(spread, axis=1)
    weight_grad = lax.dot_general(
        part_slots, spread, (((0,), (0,)), ((), ())), preferred_element_type=F32
    ).astype(BF16)
    return (hidden_grad, weight_grad)


def solution(mesh):
    placed = (
        P(("dp", "vocab"), None),
        P(None, "vocab"),
        P(("dp", "vocab"), None),
        P(("dp", "vocab"), None, None),
        P(("dp", "vocab"), None, None),
        P(("dp", "vocab")),
        P(("dp", "vocab")),
        P(("dp", "vocab")),
        P(("dp", "vocab")),
    )
    return jax.shard_map(
        body,
        mesh=mesh,
        in_specs=placed,
        out_specs=(P(("dp", "vocab"), None), P("dp", "vocab")),
        check_vma=False,
    )
```

profile of v0, /device:TPU:0, one launch (start us, length us, event | category | flops | bytes accessed | tf_op | source)
XLA Modules:
  0.0 244.4 jit_solution(17321458530008942813)
XLA Ops:
  8.0 1.3 copy.20
  9.3 32.0 %all_to_all.16 = bf16[128,4,1024]{2,0,1:T(8,128)(2,1)} all-to-all(bf16[128,4,1024]{2,0,1:T(8,128)(2,1)S(1)} %bitcast.55), channel_id=1, replica_groups=mesh['dp'=4,'vocab'=8] {'dp'}, dimensions={1} | all-to-all | bytes 2097152 | tf_op jit(solution)/shard_map/all_to_all | solution.py:48
  41.7 40.7 %all-gather.3 = bf16[32,19,128]{2,1,0:T(8,128)(2,1)S(1)} all-gather(bf16[1,19,128]{2,1,0:T(8,128)(2,1)S(1)} %bitcast.56), channel_id=2, replica_groups=mesh['dp'=4,'vocab'=8] {'dp','vocab'}, dimensions={0}, use_global_device_ids=true | all-gather | bytes 160512 | tf_op jit(solution)/shard_map/all_gather | solution.py:45
  84.4 4.6 %convolution_convert_fusion.2 = bf16[8,64,4096]{2,1,0:T(8,128)(2,1)S(1)} fusion(bf16[8,128,4096]{2,1,0:T(8,128)(2,1)} %bitcast.48, pred[32,64,128]{2,1,0:T(32,128)(4,1)S(1)} %broadcast_compare_fusion, s32[]{:T(128)S(6)} %select_n.256), kind=kOutput, calls=%fused_computation.2 | convolution fusion | flops 538968064 | bytes 12648452 | tf_op jit(solution)/shard_map/sct,sth->sch/dot_general | solution.py:82
  89.1 8.7 %multiply_convert_fusion = bf16[512,1024]{1,0:T(8,128)(2,1)S(1)} fusion(bf16[512,4096]{1,0:T(8,128)(2,1)S(1)} %bitcast.49, bf16[4096,1024]{1,0:T(8,128)(2,1)} %param.10, f32[1024]{0:T(1024)S(1)} %get-tuple-element.78, f32[512]{0:T(512)S(1)} %bitcast.61, f32[1024]{0:T(1024)S(1)} %get-tuple-element.77, f32[512]{0:T(512)S(1)} %bitcast.64, f32[512]{0:T(512)S(1)} %bitcast.60, ...), kind=kOutput, calls=%fused_computation.8 | convolution fusion | flops 4304404480 | bytes 13651968 | tf_op jit(solution)/shard_map/dot_general | solution.py:84
  97.8 0.8 select_select_fusion
  98.5 0.8 select_select_fusion.1
  99.3 0.8 select_select_fusion.2
  100.1 0.8 pad_maximum_fusion
  101.1 8.2 %convolution_convert_fusion.1 = bf16[512,4096]{1,0:T(8,128)(2,1)S(1)} fusion(bf16[512,1024]{1,0:T(8,128)(2,1)S(1)} %multiply_convert_fusion, bf16[4096,1024]{1,0:T(8,128)(2,1)} %param.10), kind=kOutput, calls=%fused_computation.1 | convolution fusion | flops 4297064448 | bytes 13631488 | tf_op jit(solution)/shard_map/dot_general | solution.py:107
  109.3 5.6 %convolution_convert_fusion = bf16[8,128,4096]{2,1,0:T(8,128)(2,1)} fusion(bf16[8,64,4096]{2,1,0:T(8,128)(2,1)S(1)} %bitcast.52, pred[32,64,128]{2,1,0:T(32,128)(4,1)S(1)} %broadcast_compare_fusion, s32[]{:T(128)S(6)} %select_n.256), kind=kOutput, calls=%fused_computation | convolution fusion | flops 541065216 | bytes 12648452 | tf_op jit(solution)/shard_map/sct,sch->sth/dot_general | solution.py:110
  115.7 8.7 %all-gather.12.cloned.1.call-done = bf16[4,1024,1024]{2,1,0:T(8,128)(2,1)} async-done(((bf16[4,128,1024]{2,1,0:T(8,128)(2,1)}), bf16[4,1024,1024]{2,1,0:T(8,128)(2,1)}) %all-gather.12.cloned.1.call-update) | async-done | bytes 8388624 | tf_op jit(solution)/shard_map/all_gather | solution.py:49
  124.4 6.6 %convolution_convert_fusion.3 = bf16[32,64,1024]{2,1,0:T(8,128)(2,1)} fusion(bf16[32,128,1024]{2,1,0:T(8,128)(2,1)} %bitcast.50, f32[32,128]{1,0:T(8,128)S(1)} %convolution_select_fusion, f32[64]{0:T(128)S(1)} %iota_convert_fusion), kind=kOutput, calls=%fused_computation.3 | convolution fusion | flops 539230208 | bytes 12599552 | tf_op jit(solution)/shard_map/sct,sth->sch/dot_general | solution.py:117
  131.0 32.6 %all-gather.8.cloned.1.call-done = bf16[2048,384]{1,0:T(8,128)(2,1)} async-done(((bf16[512,384]{1,0:T(8,128)(2,1)}), bf16[2048,384]{1,0:T(8,128)(2,1)}) %all-gather.8.cloned.1.call-update) | async-done | bytes 1572880 | tf_op jit(solution)/shard_map/all_gather | solution.py:106
  163.6 3.5 %select_dynamic-update-slice_fusion.7 = bf16[2048,1024]{1,0:T(8,128)(2,1)S(1)} fusion(pred[2048]{0:T(1024)(128)(4,1)S(1)} %get-tuple-element.58, pred[2048]{0:T(1024)(128)(4,1)S(1)} %get-tuple-element.57, pred[2048]{0:T(1024)(128)(4,1)S(1)} %get-tuple-element.56, bf16[2048,384]{1,0:T(8,128)(2,1)} %all-gather.8.cloned.1.call-done), kind=kLoop, calls=%fused_computation.22 | loop fusion | flops 786431 | bytes 2103296
  167.1 3.4 %select_dynamic-update-slice_fusion.6 = bf16[2048,1024]{1,0:T(8,128)(2,1)S(1)} fusion(bf16[2048,1024]{1,0:T(8,128)(2,1)S(1)} %select_dynamic-update-slice_fusion.7, pred[2048]{0:T(1024)(128)(4,1)S(1)} %get-tuple-element.16, pred[2048]{0:T(1024)(128)(4,1)S(1)} %get-tuple-element.9, pred[2048]{0:T(1024)(128)(4,1)S(1)} %get-tuple-element.3, ...), kind=kLoop, calls=%fused_computation.21 | loop fusion | flops 786432 | bytes 2103296
  170.5 1.8 select_dynamic-update-slice_fusion.5
  172.3 1.8 select_dynamic-update-slice_fusion.4
  174.1 1.8 select_dynamic-update-slice_fusion.3
  175.9 1.8 select_dynamic-update-slice_fusion.2
  177.6 1.8 select_dynamic-update-slice_fusion.1
  179.4 1.8 select_dynamic-update-slice_fusion
  181.2 5.7 %convolution_convert_fusion.4 = bf16[1024,1024]{1,0:T(8,128)(2,1)} fusion(bf16[2048,1024]{1,0:T(8,128)(2,1)S(1)} %bitcast.51, bf16[2048,1024]{1,0:T(8,128)(2,1)S(1)} %select_dynamic-update-slice_fusion), kind=kOutput, calls=%fused_computation.9 | convolution fusion | flops 4296015872 | bytes 10485760 | tf_op jit(solution)/shard_map/dot_general | solution.py:135
  187.0 50.9 %reduce-scatter.2.cloned.1.call-done = bf16[128,4096]{1,0:T(8,128)(2,1)} async-done(((bf16[1024,4096]{1,0:T(8,128)(2,1)}), bf16[128,4096]{1,0:T(8,128)(2,1)}) %reduce-scatter.2.cloned.1.call-update) | async-done | bytes 1048592 | tf_op jit(solution)/shard_map/reduce_scatter | solution.py:113
  (54 shorter events, 4.0 us)
Async XLA Ops:
  7.2 34.2 %copy-start.2 = (s32[128,3,2]{0,2,1:T(2,128)S(1)}, s32[128,3,2]{0,2,1:T(2,128)}, u32[]{:S(2)}) copy-start(s32[128,3,2]{0,2,1:T(2,128)} %param.12) | copy-start | bytes 9220
  7.2 34.3 %copy-start.3 = (s32[128,3,2]{0,2,1:T(2,128)S(1)}, s32[128,3,2]{0,2,1:T(2,128)}, u32[]{:S(2)}) copy-start(s32[128,3,2]{0,2,1:T(2,128)} %param.13) | copy-start | bytes 9220
  7.2 34.3 %copy-start.5 = (s32[128]{0:T(128)S(1)}, s32[128]{0:T(128)}, u32[]{:S(2)}) copy-start(s32[128]{0:T(128)} %param.15) | copy-start | bytes 1540
  7.2 34.3 %copy-start.6 = (s32[128]{0:T(128)S(1)}, s32[128]{0:T(128)}, u32[]{:S(2)}) copy-start(s32[128]{0:T(128)} %param.14) | copy-start | bytes 1540
  7.2 34.3 %copy-start.4 = (s32[128,3]{0,1:T(4,128)S(1)}, s32[128,3]{0,1:T(4,128)}, u32[]{:S(2)}) copy-start(s32[128,3]{0,1:T(4,128)} %param.11) | copy-start | bytes 4612
  7.2 34.3 %copy-start.7 = (bf16[128]{0:T(256)(128)(2,1)S(1)}, bf16[128]{0:T(256)(128)(2,1)}, u32[]{:S(2)}) copy-start(bf16[128]{0:T(256)(128)(2,1)} %param.16) | copy-start | bytes 772
  7.2 34.3 %copy-start.8 = (bf16[128]{0:T(256)(128)(2,1)S(1)}, bf16[128]{0:T(256)(128)(2,1)}, u32[]{:S(2)}) copy-start(bf16[128]{0:T(256)(128)(2,1)} %param.17) | copy-start | bytes 772
  7.2 77.2 %all-gather.10.cloned.1.call-start = ((), (), s32[]{:S(2)}) async-start(), calls=%async_computation.4 | async-start | bytes 9437184 | tf_op jit(solution)/shard_map/all_gather | solution.py:47
  8.0 116.4 %all-gather.12.cloned.1.call-start = ((), (), s32[]{:S(2)}) async-start(), calls=%async_computation.5 | async-start | bytes 9437184 | tf_op jit(solution)/shard_map/all_gather | solution.py:49
  41.3 122.3 %all-gather.8.cloned.1.call-start = ((), (), s32[]{:S(2)}) async-start(), calls=%async_computation.3 | async-start | bytes 1966080 | tf_op jit(solution)/shard_map/all_gather | solution.py:106
  100.9 137.0 %reduce-scatter.2.cloned.1.call-start = ((), (), s32[]{:S(2)}) async-start(), calls=%async_computation.2 | async-start | bytes 9437184 | tf_op jit(solution)/shard_map/reduce_scatter | solution.py:113
  163.6 6.9 %copy-start = (bf16[2048,384]{1,0:T(8,128)(2,1)S(1)}, bf16[2048,384]{1,0:T(8,128)(2,1)}, u32[]{:S(2)}) copy-start(bf16[2048,384]{1,0:T(8,128)(2,1)} %all-gather.8.cloned.1.call-done) | copy-start | bytes 4718596
  174.1 7.1 %copy-start.1 = (bf16[32,64,1024]{2,1,0:T(8,128)(2,1)S(1)}, bf16[32,64,1024]{2,1,0:T(8,128)(2,1)}, u32[]{:S(2)}) copy-start(bf16[32,64,1024]{2,1,0:T(8,128)(2,1)} %convolution_convert_fusion.3) | copy-start | bytes 12582916
Sparse Core Ops, SparseCore 0:
  9.9 58.0 all-gather.9
  70.0 54.3 all-gather.11
  126.5 37.0 all-gather.7
  167.5 70.3 reduce-scatter.1
where the time goes:
time: 245 us; the launch traced here: 244 us
  waiting for transfers between devices  93 us (38%)
  blocking collectives  72.6 us (30%)
  matrix products  40 us (16%)
  other arithmetic  22 us (9%)
  between operations  14.2 us (6%)
    reduce_scatter x1, waiting for transfers between devices, body(): lax.psum_scatter(back.reshape(n_vocab * tokens, width), 'vocab', scatter_...  50.9 us
    all_gather x1, blocking collectives, body(): facts = lax.all_gather(facts, ('dp', 'vocab'), axis=0, tiled=False)  40.7 us
    all_gather x1, waiting for transfers between devices, body(): packed = lax.all_gather(packed, 'dp', axis=0, tiled=True)  32.6 us
    all_to_all x1, blocking collectives, body(): lax.all_to_all(hidden, 'dp', split_axis=1, concat_axis=0, tiled=True)  32 us
    unnamed x7, other arithmetic  15.7 us
    all_gather x1, waiting for transfers between devices, body(): lax.all_gather(part_rows.reshape(n_dp, tokens, part), 'vocab', axis=1)  8.72 us
    dot_general x1, matrix products, body(): scores = jnp.dot(rows, output_weight, preferred_element_type=F32)  8.7 us
    dot_general x1, matrix products, body(): lax.dot_general(grad, output_weight, (((1,), (1,)), ((), ())), preferred_...  8.19 us
  transfers between devices with their start and end apart: 4, of which 3 were waited for; matrix products, arithmetic and copies ran while one was open for 26% of the time, Pallas kernels for 0%

commit v1 on v0

--- a/solution.py
+++ b/solution.py
@@ -7,6 +7,18 @@
 BLK_DEV = 8
 F32 = jnp.float32
 BF16 = jnp.bfloat16
+
+
+def doubled_up(value, axis, dim):
+    ways, here = (lax.axis_size(axis), lax.axis_index(axis))
+    grown, reach = (value, 1)
+    while reach < ways:
+        theirs = lax.ppermute(grown, axis, [(d, d ^ reach) for d in range(ways)])
+        mine_first = jnp.concatenate([grown, theirs], axis=dim)
+        theirs_first = jnp.concatenate([theirs, grown], axis=dim)
+        grown = jnp.where(here & reach == 0, mine_first, theirs_first)
+        reach = 2 * reach
+    return grown
 
 
 def body(
@@ -103,7 +115,7 @@
             value = jnp.where(which == b + 1.0, grad[:, b * BLOCK : (b + 1) * BLOCK], value)
         packed.append(value)
     packed = jnp.concatenate(packed, axis=1)
-    packed = lax.all_gather(packed, "dp", axis=0, tiled=True)
+    packed = doubled_up(packed, "dp", 0)
     back = lax.dot_general(
         grad, output_weight, (((1,), (1,)), ((), ())), preferred_element_type=F32
     ).astype(BF16)

time: 245 us -> 207 us (0.84)
  waiting for transfers between devices: 93 us -> 54.6 us
  other arithmetic: 22 us -> 25.4 us
  matrix products: 40 us -> 37.3 us
    ppermute x0 -> x2, waiting for transfers between devices: none -> 47.4 us  [doubled_up(): theirs = lax.ppermute(grown, axis, [(d, d ^ reach) for d in range(ways)])]
    reduce_scatter x1, waiting for transfers between devices: 50.9 us -> 6.41 us  [body(): lax.psum_scatter(back.reshape(n_vocab * tokens, width), 'vocab', scatter_...]
    all_gather x1 -> x0, waiting for transfers between devices: 32.6 us -> none  [body(): packed = lax.all_gather(packed, 'dp', axis=0, tiled=True)]
    all_gather x1, waiting for transfers between devices: 8.72 us -> 0.01 us  [body(): lax.all_gather(part_rows.reshape(n_dp, tokens, part), 'vocab', axis=1)]
    dot_general x1, matrix products: 8.19 us -> 4.8 us  [body(): lax.dot_general(grad, output_weight, (((1,), (1,)), ((), ())), preferred_...]
    unnamed x7 -> x8, other arithmetic: 15.7 us -> 18.2 us
  transfers between devices with their start and end apart: 4 -> 5, of which waited for: 3 -> 3; matrix products, arithmetic and copies ran while one was open for 26% -> 31% of each run, Pallas kernels for 0% -> 0%
where the time goes in v1:
time: 207 us; the launch traced here: 206 us
  blocking collectives  72.6 us (35%)
  waiting for transfers between devices  54.6 us (26%)
  matrix products  37.3 us (18%)
  other arithmetic  25.4 us (12%)
  between operations  14.1 us (7%)
  local copies, waits for them, and re-layouts  2.19 us (1%)
    ppermute x2, waiting for transfers between devices, doubled_up(): theirs = lax.ppermute(grown, axis, [(d, d ^ reach) for d in range(ways)])  47.4 us
    all_gather x1, blocking collectives, body(): facts = lax.all_gather(facts, ('dp', 'vocab'), axis=0, tiled=False)  40.7 us
    all_to_all x1, blocking collectives, body(): lax.all_to_all(hidden, 'dp', split_axis=1, concat_axis=0, tiled=True)  32 us
    unnamed x8, other arithmetic  18.2 us
    dot_general x1, matrix products, body(): scores = jnp.dot(rows, output_weight, preferred_element_type=F32)  8.85 us
    dot_general x1, matrix products, body(): lax.dot_general(part_slots, spread, (((0,), (0,)), ((), ())), preferred_e...  8.01 us
    reduce_scatter x1, waiting for transfers between devices, body(): lax.psum_scatter(back.reshape(n_vocab * tokens, width), 'vocab', scatter_...  6.41 us
    dot_general x1, matrix products, body(): jnp.einsum('sct,sch->sth', my_pick, back.reshape(n_vocab, capacity, width...  5.59 us
  transfers between devices with their start and end apart: 5, of which 3 were waited for; matrix products, arithmetic and copies ran while one was open for 31% of the time, Pallas kernels for 0%

profile of v1, /device:TPU:0, one launch (start us, length us, event | category | flops | bytes accessed | tf_op | source)
XLA Modules:
  0.0 206.5 jit_solution(9491375771601144752)
XLA Ops:
  7.3 0.7 all-gather.7.cloned.1.call-update
  8.0 1.3 copy.20
  9.3 32.0 %all_to_all.16 = bf16[128,4,1024]{2,0,1:T(8,128)(2,1)} all-to-all(bf16[128,4,1024]{2,0,1:T(8,128)(2,1)S(1)} %bitcast.55), channel_id=1, replica_groups=mesh['dp'=4,'vocab'=8] {'dp'}, dimensions={1} | all-to-all | bytes 2097152 | tf_op jit(solution)/shard_map/all_to_all | solution.py:60
  41.7 40.7 %all-gather.3 = bf16[32,19,128]{2,1,0:T(8,128)(2,1)S(1)} all-gather(bf16[1,19,128]{2,1,0:T(8,128)(2,1)S(1)} %bitcast.56), channel_id=2, replica_groups=mesh['dp'=4,'vocab'=8] {'dp','vocab'}, dimensions={0}, use_global_device_ids=true | all-gather | bytes 160512 | tf_op jit(solution)/shard_map/all_gather | solution.py:57
  84.3 4.8 %convolution_convert_fusion.2 = bf16[8,64,4096]{2,1,0:T(8,128)(2,1)S(1)} fusion(bf16[8,128,4096]{2,1,0:T(8,128)(2,1)} %bitcast.48, pred[32,64,128]{2,1,0:T(32,128)(4,1)S(1)} %broadcast_compare_fusion, s32[]{:T(128)S(6)} %select_n.272), kind=kOutput, calls=%fused_computation.2 | convolution fusion | flops 538968064 | bytes 12648452 | tf_op jit(solution)/shard_map/sct,sth->sch/dot_general | solution.py:94
  89.1 8.8 %multiply_convert_fusion = bf16[512,1024]{1,0:T(8,128)(2,1)S(1)} fusion(bf16[512,4096]{1,0:T(8,128)(2,1)S(1)} %bitcast.49, bf16[4096,1024]{1,0:T(8,128)(2,1)} %param.10, f32[1024]{0:T(1024)S(1)} %get-tuple-element.78, f32[512]{0:T(512)S(1)} %bitcast.61, f32[1024]{0:T(1024)S(1)} %get-tuple-element.77, f32[512]{0:T(512)S(1)} %bitcast.64, f32[512]{0:T(512)S(1)} %bitcast.60, ...), kind=kOutput, calls=%fused_computation.8 | convolution fusion | flops 4304404480 | bytes 13651968 | tf_op jit(solution)/shard_map/dot_general | solution.py:96
  98.0 4.8 %convolution_convert_fusion.1 = bf16[512,4096]{1,0:T(8,128)(2,1)S(1)} fusion(bf16[512,1024]{1,0:T(8,128)(2,1)S(1)} %multiply_convert_fusion, bf16[4096,1024]{1,0:T(8,128)(2,1)S(1)} %bitcast.68), kind=kOutput, calls=%fused_computation.1 | convolution fusion | flops 4297064448 | bytes 13631488 | tf_op jit(solution)/shard_map/dot_general | solution.py:119
  102.8 5.6 %convolution_convert_fusion = bf16[8,128,4096]{2,1,0:T(8,128)(2,1)} fusion(bf16[8,64,4096]{2,1,0:T(8,128)(2,1)S(1)} %bitcast.52, pred[32,64,128]{2,1,0:T(32,128)(4,1)S(1)} %broadcast_compare_fusion, s32[]{:T(128)S(6)} %select_n.272), kind=kOutput, calls=%fused_computation | convolution fusion | flops 541065216 | bytes 12648452 | tf_op jit(solution)/shard_map/sct,sch->sth/dot_general | solution.py:122
  108.5 0.8 select_select_fusion
  109.3 0.8 select_select_fusion.1
  110.1 0.9 select_select_fusion.2
  111.2 11.3 %collective-permute-done = bf16[512,384]{1,0:T(8,128)(2,1)S(1)} collective-permute-done((bf16[512,384]{1,0:T(8,128)(2,1)S(1)}, bf16[512,384]{1,0:T(8,128)(2,1)S(1)}, u32[]{:S(2)}, u32[]{:S(2)}) %collective-permute-start) | collective-permute-done | bytes 393248 | tf_op jit(solution)/shard_map/ppermute | solution.py:16
  123.6 36.1 %collective-permute-done.1 = bf16[1024,384]{1,0:T(8,128)(2,1)S(1)} collective-permute-done((bf16[1024,384]{1,0:T(8,128)(2,1)S(1)}, bf16[1024,384]{1,0:T(8,128)(2,1)S(1)}, u32[]{:S(2)}, u32[]{:S(2)}) %collective-permute-start.1) | collective-permute-done | bytes 786464 | tf_op jit(solution)/shard_map/ppermute | solution.py:16
  160.1 2.6 %select_dynamic-update-slice_fusion.7 = bf16[2048,1024]{1,0:T(8,128)(2,1)} fusion(pred[2048]{0:T(1024)(128)(4,1)S(1)} %get-tuple-element.58, pred[2048]{0:T(1024)(128)(4,1)S(1)} %get-tuple-element.57, pred[2048]{0:T(1024)(128)(4,1)S(1)} %get-tuple-element.56, bf16[2048,384]{1,0:T(8,128)(2,1)S(1)} %maximum_select_fusion), kind=kLoop, calls=%fused_computation.24 | loop fusion | flops 786431 | bytes 2103296
  162.7 2.6 %select_dynamic-update-slice_fusion.6 = bf16[2048,1024]{1,0:T(8,128)(2,1)} fusion(bf16[2048,1024]{1,0:T(8,128)(2,1)} %select_dynamic-update-slice_fusion.7, pred[2048]{0:T(1024)(128)(4,1)S(1)} %get-tuple-element.16, pred[2048]{0:T(1024)(128)(4,1)S(1)} %get-tuple-element.9, pred[2048]{0:T(1024)(128)(4,1)S(1)} %get-tuple-element.3, ...), kind=kLoop, calls=%fused_computation.23 | loop fusion | flops 786432 | bytes 2103296
  165.3 2.6 %select_dynamic-update-slice_fusion.5 = bf16[2048,1024]{1,0:T(8,128)(2,1)} fusion(bf16[2048,1024]{1,0:T(8,128)(2,1)} %select_dynamic-update-slice_fusion.6, pred[2048]{0:T(1024)(128)(4,1)S(1)} %get-tuple-element.17, pred[2048]{0:T(1024)(128)(4,1)S(1)} %get-tuple-element.10, pred[2048]{0:T(1024)(128)(4,1)S(1)} %get-tuple-element.4, ...), kind=kLoop, calls=%fused_computation.22 | loop fusion | flops 786432 | bytes 2103296
  167.9 2.6 %select_dynamic-update-slice_fusion.4 = bf16[2048,1024]{1,0:T(8,128)(2,1)} fusion(bf16[2048,1024]{1,0:T(8,128)(2,1)} %select_dynamic-update-slice_fusion.5, pred[2048]{0:T(1024)(128)(4,1)S(1)} %get-tuple-element.18, pred[2048]{0:T(1024)(128)(4,1)S(1)} %get-tuple-element.11, pred[2048]{0:T(1024)(128)(4,1)S(1)} %get-tuple-element.5, ...), kind=kLoop, calls=%fused_computation.21 | loop fusion | flops 786432 | bytes 2103296
  170.5 2.6 %select_dynamic-update-slice_fusion.3 = bf16[2048,1024]{1,0:T(8,128)(2,1)} fusion(bf16[2048,1024]{1,0:T(8,128)(2,1)} %select_dynamic-update-slice_fusion.4, pred[2048]{0:T(1024)(128)(4,1)S(1)} %get-tuple-element.19, pred[2048]{0:T(1024)(128)(4,1)S(1)} %get-tuple-element.12, pred[2048]{0:T(1024)(128)(4,1)S(1)} %get-tuple-element.6, ...), kind=kLoop, calls=%fused_computation.20 | loop fusion | flops 786432 | bytes 2103296
  173.1 2.6 %select_dynamic-update-slice_fusion.2 = bf16[2048,1024]{1,0:T(8,128)(2,1)} fusion(bf16[2048,1024]{1,0:T(8,128)(2,1)} %select_dynamic-update-slice_fusion.3, pred[2048]{0:T(1024)(128)(4,1)S(1)} %get-tuple-element.20, pred[2048]{0:T(1024)(128)(4,1)S(1)} %get-tuple-element.13, pred[2048]{0:T(1024)(128)(4,1)S(1)} %get-tuple-element.7, ...), kind=kLoop, calls=%fused_computation.19 | loop fusion | flops 786432 | bytes 2103296
  175.7 2.6 %select_dynamic-update-slice_fusion.1 = bf16[2048,1024]{1,0:T(8,128)(2,1)} fusion(bf16[2048,1024]{1,0:T(8,128)(2,1)} %select_dynamic-update-slice_fusion.2, pred[2048]{0:T(1024)(128)(4,1)S(1)} %get-tuple-element.59, pred[2048]{0:T(1024)(128)(4,1)S(1)} %get-tuple-element.14, pred[2048]{0:T(1024)(128)(4,1)S(1)} %get-tuple-element.8, ...), kind=kLoop, calls=%fused_computation.18 | loop fusion | flops 786432 | bytes 2103296
  178.3 2.6 %select_dynamic-update-slice_fusion = bf16[2048,1024]{1,0:T(8,128)(2,1)} fusion(bf16[2048,1024]{1,0:T(8,128)(2,1)} %select_dynamic-update-slice_fusion.1, pred[2048]{0:T(1024)(128)(4,1)S(1)} %get-tuple-element.60, pred[2048]{0:T(1024)(128)(4,1)S(1)} %get-tuple-element.15, pred[2048]{0:T(1024)(128)(4,1)S(1)} %get-tuple-element.2, ...), kind=kLoop, calls=%fused_computation.17 | loop fusion | flops 786432 | bytes 2103296 | tf_op jit(solution)/shard_map/concatenate | solution.py:146
  180.9 4.7 %convolution_convert_fusion.3 = bf16[32,64,1024]{2,1,0:T(8,128)(2,1)S(1)} fusion(bf16[32,128,1024]{2,1,0:T(8,128)(2,1)} %bitcast.50, f32[32,128]{1,0:T(8,128)S(1)} %convolution_select_fusion, f32[64]{0:T(128)S(1)} %iota_convert_fusion), kind=kOutput, calls=%fused_computation.3 | convolution fusion | flops 539230208 | bytes 12599552 | tf_op jit(solution)/shard_map/sct,sth->sch/dot_general | solution.py:129
  185.5 8.0 %convolution_convert_fusion.4 = bf16[1024,1024]{1,0:T(8,128)(2,1)} fusion(bf16[2048,1024]{1,0:T(8,128)(2,1)S(1)} %bitcast.51, bf16[2048,1024]{1,0:T(8,128)(2,1)} %select_dynamic-update-slice_fusion), kind=kOutput, calls=%fused_computation.9 | convolution fusion | flops 4296015872 | bytes 10485760 | tf_op jit(solution)/shard_map/dot_general | solution.py:147
  193.6 6.4 %reduce-scatter.2.cloned.1.call-done = bf16[128,4096]{1,0:T(8,128)(2,1)} async-done(((bf16[1024,4096]{1,0:T(8,128)(2,1)}), bf16[128,4096]{1,0:T(8,128)(2,1)}) %reduce-scatter.2.cloned.1.call-update) | async-done | bytes 1048592 | tf_op jit(solution)/shard_map/reduce_scatter | solution.py:125
  (58 shorter events, 3.9 us)
Async XLA Ops:
  7.2 34.2 %copy-start = (s32[128,3,2]{0,2,1:T(2,128)S(1)}, s32[128,3,2]{0,2,1:T(2,128)}, u32[]{:S(2)}) copy-start(s32[128,3,2]{0,2,1:T(2,128)} %param.12) | copy-start | bytes 9220
  7.2 34.3 %copy-start.1 = (s32[128,3,2]{0,2,1:T(2,128)S(1)}, s32[128,3,2]{0,2,1:T(2,128)}, u32[]{:S(2)}) copy-start(s32[128,3,2]{0,2,1:T(2,128)} %param.13) | copy-start | bytes 9220
  7.2 34.3 %copy-start.3 = (s32[128]{0:T(128)S(1)}, s32[128]{0:T(128)}, u32[]{:S(2)}) copy-start(s32[128]{0:T(128)} %param.15) | copy-start | bytes 1540
  7.2 34.3 %copy-start.4 = (s32[128]{0:T(128)S(1)}, s32[128]{0:T(128)}, u32[]{:S(2)}) copy-start(s32[128]{0:T(128)} %param.14) | copy-start | bytes 1540
  7.2 34.3 %copy-start.2 = (s32[128,3]{0,1:T(4,128)S(1)}, s32[128,3]{0,1:T(4,128)}, u32[]{:S(2)}) copy-start(s32[128,3]{0,1:T(4,128)} %param.11) | copy-start | bytes 4612
  7.2 34.3 %copy-start.5 = (bf16[128]{0:T(256)(128)(2,1)S(1)}, bf16[128]{0:T(256)(128)(2,1)}, u32[]{:S(2)}) copy-start(bf16[128]{0:T(256)(128)(2,1)} %param.16) | copy-start | bytes 772
  7.2 34.3 %copy-start.6 = (bf16[128]{0:T(256)(128)(2,1)S(1)}, bf16[128]{0:T(256)(128)(2,1)}, u32[]{:S(2)}) copy-start(bf16[128]{0:T(256)(128)(2,1)} %param.17) | copy-start | bytes 772
  7.2 77.0 %all-gather.7.cloned.1.call-start = ((), (), s32[]{:S(2)}) async-start(), calls=%async_computation.3 | async-start | bytes 9437184 | tf_op jit(solution)/shard_map/all_gather | solution.py:59
  8.0 172.9 %all-gather.9.cloned.1.call-start = ((), (), s32[]{:S(2)}) async-start(), calls=%async_computation.4 | async-start | bytes 9437184 | tf_op jit(solution)/shard_map/all_gather | solution.py:61
  41.3 158.6 %reduce-scatter.2.cloned.1.call-start = ((), (), s32[]{:S(2)}) async-start(), calls=%async_computation.2 | async-start | bytes 9437184 | tf_op jit(solution)/shard_map/reduce_scatter | solution.py:125
  84.3 13.7 %slice-start = ((s8[8388608]{0:T(1024)(128)(4,1)}), s8[4194304]{0:T(1024)(128)(4,1)S(1)}, s32[]{:S(2)}) async-start(s8[8388608]{0:T(1024)(128)(4,1)} %bitcast.67), calls=%async_computation.5 | async-start | bytes 8388608
  89.1 8.9 %slice-start.1 = ((s8[8388608]{0:T(1024)(128)(4,1)}), s8[4194304]{0:T(1024)(128)(4,1)S(1)}, s32[]{:S(2)}) async-start(s8[8388608]{0:T(1024)(128)(4,1)} %bitcast.67), calls=%async_computation.6 | async-start | bytes 8388608
  111.1 11.4 %collective-permute-start = (bf16[512,384]{1,0:T(8,128)(2,1)S(1)}, bf16[512,384]{1,0:T(8,128)(2,1)S(1)}, u32[]{:S(2)}, u32[]{:S(2)}) collective-permute-start(bf16[512,384]{1,0:T(8,128)(2,1)S(1)} %pad_maximum_fusion), channel_id=1, source_target_pairs={{0,8},{8,0},{16,24},{24,16},{1,9},{9,1},{17,25},{25,17},{2,10},{10... | collective-permute-start | bytes 1179656 | tf_op jit(solution)/shard_map/ppermute | solution.py:16
  122.8 36.9 %collective-permute-start.1 = (bf16[1024,384]{1,0:T(8,128)(2,1)S(1)}, bf16[1024,384]{1,0:T(8,128)(2,1)S(1)}, u32[]{:S(2)}, u32[]{:S(2)}) collective-permute-start(bf16[1024,384]{1,0:T(8,128)(2,1)S(1)} %maximum_select_fusion.1), channel_id=1, source_target_pairs={{0,16},{8,24},{16,0},{24,8},{1,17},{9,25},{17,1},{25,9},{2,18},{10... | collective-permute-start | bytes 2359304 | tf_op jit(solution)/shard_map/ppermute | solution.py:16
Sparse Core Ops, SparseCore 0:
  9.9 58.0 all-gather.6
  70.0 54.3 all-gather.8
  128.4 71.4 reduce-scatter.1
